TPU v7x, 32 devices: a whole 2x2x4 slice. The times are simulated.
32 devices in a mesh: block: 4 (over y, x), tok: 8 (over z, core).
Axes of the slice: x: 2, y: 2, z: 4, core: 2. Of those that a mesh axis runs over, the one named last changes fastest.
Arguments:
- queries: float32 [4096, 256], P(('block', 'tok')), may hold values from -6 to 6
- keys: float32 [4096, 256], P(('block', 'tok')), may hold values from -6 to 6
- values: float32 [4096, 256], P(('block', 'tok')), may hold values from -6 to 6
- rates: float32 [4096], P(('block', 'tok')), may hold values from 0.0001 to 0.001
- states: float32 [4, 3, 256, 256], P('block', None, 'tok'), may hold values from -0.375 to 0.375
- out_cot: float32 [4096, 256], P(('block', 'tok')), may hold values from -6 to 6
- final_cot: float32 [3, 256, 256], P(None, 'tok'), may hold values from -6 to 6
Outputs:
- d_queries: float32 [4096, 256], P(('block', 'tok'))
- d_keys: float32 [4096, 256], P(('block', 'tok'))
- d_values: float32 [4096, 256], P(('block', 'tok'))
- d_rates: float32 [4096], P(('block', 'tok'))
- d_states: float32 [4, 3, 256, 256], P('block', None, 'tok')
All inputs are finite; a program needn't handle non-finite values.
Results may differ from a plain program's by a relative error of at most 0.00029.
Values sent between devices are 32-bit elements; how exact they have to be, the bound alone decides.
No kernel may reach another device: no remote copies, remote signals or barrier semaphores. Data moves between devices by JAX's collectives and lax.ppermute only.
A program may use at most 64 MiB of HBM per device.

v0:
```python
import jax
import jax.numpy as jnp
from jax import lax
from jax.sharding import PartitionSpec as P

EPS = 1e-06
HIGH = lax.Precision.HIGHEST


def from_behind(array, axis, by):
    devices = lax.axis_size(axis)
    pairs = [(i, i + by) for i in range(devices) if 0 <= i + by < devices]
    return lax.ppermute(array, axis, pairs)


def apply_fast(weights, inputs):
    first = jnp.dot(inputs, weights[0], precision=HIGH, preferred_element_type=jnp.float32)
    gate = jnp.dot(inputs, weights[1], precision=HIGH, preferred_element_type=jnp.float32)
    mixed = jax.nn.silu(first) * gate
    return jnp.dot(mixed, weights[2], precision=HIGH, preferred_element_type=jnp.float32)


def update_grad(weights, keys, values, rates):

    def loss(current):
        return -jnp.sum(rates[:, None] * apply_fast(current, keys) * values)

    return jax.grad(loss)(weights)


def norm_adjoint(incoming, shifted, own, row_norm, new_norm):
    inner = jnp.sum(incoming * shifted, axis=-1, keepdims=True)
    d_shifted = (
        row_norm / new_norm * incoming
        - row_norm * inner / (new_norm * new_norm * new_norm) * shifted
    )
    direct = d_shifted + inner / new_norm * own / row_norm
    return (d_shifted, direct)


def per_device(queries, keys, values, rates, states, out_cot, final_cot):
    groups = lax.axis_size("block")
    position = lax.axis_index("block")
    own_rows = states[0]
    gathered = lax.all_gather(own_rows, "tok", axis=1, tiled=True)
    _, apply_back = jax.vjp(apply_fast, gathered, queries)
    apply_state, d_queries = apply_back(out_cot)
    grad_part, second_back = jax.vjp(update_grad, gathered, keys, values, rates)
    grad_rows = lax.psum_scatter(grad_part, "tok", scatter_dimension=1, tiled=True)
    shifted = own_rows - grad_rows
    row_norm = jnp.sqrt(jnp.sum(own_rows * own_rows, axis=-1, keepdims=True) + EPS)
    new_norm = jnp.sqrt(jnp.sum(shifted * shifted, axis=-1, keepdims=True) + EPS)
    zero_back = (
        jnp.zeros_like(gathered),
        jnp.zeros_like(keys),
        jnp.zeros_like(values),
        jnp.zeros_like(rates),
    )
    incoming = final_cot
    d_keys = jnp.zeros_like(keys)
    d_values = jnp.zeros_like(values)
    d_rates = jnp.zeros_like(rates)
    d_rows = jnp.zeros_like(own_rows)
    for section in range(groups):
        active = position == groups - 1 - section
        d_shifted, direct = norm_adjoint(incoming, shifted, own_rows, row_norm, new_norm)
        d_grad = lax.all_gather(-d_shifted, "tok", axis=1, tiled=True)
        second_state, second_keys, second_values, second_rates = lax.cond(
            active, lambda cot: second_back(cot), lambda cot: zero_back, d_grad
        )
        summed = lax.psum_scatter(
            second_state + apply_state, "tok", scatter_dimension=1, tiled=True
        )
        rows_now = summed + direct
        d_keys = jnp.where(active, second_keys, d_keys)
        d_values = jnp.where(active, second_values, d_values)
        d_rates = jnp.where(active, second_rates, d_rates)
        d_rows = jnp.where(active, rows_now, d_rows)
        if section + 1 < groups:
            incoming = from_behind(rows_now, "block", -1)
    return (d_queries, d_keys, d_values, d_rates, d_rows[None])


def solution(mesh):
    return jax.shard_map(
        per_device,
        mesh=mesh,
        in_specs=(
            P(("block", "tok"), None),
            P(("block", "tok"), None),
            P(("block", "tok"), None),
            P(("block", "tok")),
            P("block", None, "tok", None),
            P(("block", "tok"), None),
            P(None, "tok", None),
        ),
        out_specs=(
            P(("block", "tok"), None),
            P(("block", "tok"), None),
            P(("block", "tok"), None),
            P(("block", "tok")),
            P("block", None, "tok", None),
        ),
        check_vma=False,
    )
```

profile of v0, /device:TPU:0, one launch (start us, length us, event | category | flops | bytes accessed | tf_op | source)
XLA Modules:
  0.0 317.6 jit_solution(9422228278440571591)
XLA Ops:
  7.2 0.7 broadcast_multiply_fusion.2
  7.9 17.5 %all-gather = f32[1,3,256,256]{3,2,1,0:T(8,128)S(1)} all-gather(f32[1,3,32,256]{3,2,1,0:T(8,128)} %param.19), channel_id=2, replica_groups=mesh['block'=4,'tok'=8] {'tok'}, dimensions={2}, use_global_device_ids=true | all-gather | bytes 884736 | tf_op jit(solution)/shard_map/all_gather | solution.py:45
  25.6 0.8 copy-done.1
  27.1 1.1 multiply_add_fusion.12
  28.2 0.4 convolution_bitcast_fusion.17
  28.6 0.4 convolution_bitcast_fusion.16
  29.1 0.4 convolution_bitcast_fusion.15
  29.5 1.0 pad_add_fusion.5
  31.1 0.6 copy-done.42
  31.7 0.4 convolution_bitcast_fusion.14
  32.6 0.4 convolution_bitcast_fusion.13
  33.2 0.4 convolution_bitcast_fusion.12
  33.7 0.9 slice_bitcast_fusion.1
  34.6 29.1 %reduce-scatter.6.cloned.1.call-done = f32[3,32,256]{2,1,0:T(8,128)} async-done(((f32[3,256,256]{2,1,0:T(8,128)}), f32[3,32,256]{2,1,0:T(8,128)}) %reduce-scatter.6.cloned.1.call-update) | async-done | bytes 98320 | tf_op jit(solution)/shard_map/reduce_scatter | solution.py:49
  63.7 1.1 multiply_reduce_fusion.8
  65.0 15.9 %all_gather.16 = f32[3,256,256]{2,1,0:T(8,128)S(1)} all-gather(f32[3,32,256]{2,1,0:T(8,128)S(1)} %fusion.92), channel_id=1, replica_groups=mesh['block'=4,'tok'=8] {'tok'}, dimensions={1}, use_global_device_ids=true | all-gather | bytes 884736 | tf_op jit(solution)/shard_map/all_gather | solution.py:67
  80.9 0.6 copy-done.44
  81.5 1.4 conditional.4
  81.5 0.7 broadcast.77.clone
  82.1 0.7 broadcast.77
  82.9 1.0 fusion.86
  83.9 35.0 %reduce-scatter.8.cloned.1.call-done = f32[3,32,256]{2,1,0:T(8,128)} async-done(((f32[3,256,256]{2,1,0:T(8,128)}), f32[3,32,256]{2,1,0:T(8,128)}) %reduce-scatter.8.cloned.1.call-update) | async-done | bytes 98320 | tf_op jit(solution)/shard_map/reduce_scatter | solution.py:71
  118.9 1.7 fusion.76
  120.6 1.3 collective-permute-start
  121.9 5.5 %collective-permute-done = f32[3,32,256]{2,1,0:T(8,128)} collective-permute-done((f32[3,32,256]{2,1,0:T(8,128)}, f32[3,32,256]{2,1,0:T(8,128)}, u32[]{:S(2)}, u32[]{:S(2)}) %collective-permute-start) | collective-permute-done | bytes 98336 | tf_op jit(solution)/shard_map/ppermute | solution.py:13
  127.4 1.0 multiply_reduce_fusion.6
  128.5 1.0 fusion.93
  129.6 15.8 %all_gather.17 = f32[3,256,256]{2,1,0:T(8,128)S(1)} all-gather(f32[3,32,256]{2,1,0:T(8,128)S(1)} %fusion.93), channel_id=1, replica_groups=mesh['block'=4,'tok'=8] {'tok'}, dimensions={1}, use_global_device_ids=true | all-gather | bytes 884736 | tf_op jit(solution)/shard_map/all_gather | solution.py:67
  145.4 1.6 conditional.5
  145.4 0.7 broadcast.85.clone
  146.1 0.7 broadcast.85
  147.0 1.0 fusion.85
  148.1 34.5 %reduce-scatter.10.cloned.1.call-done = f32[3,32,256]{2,1,0:T(8,128)} async-done(((f32[3,256,256]{2,1,0:T(8,128)}), f32[3,32,256]{2,1,0:T(8,128)}) %reduce-scatter.10.cloned.1.call-update) | async-done | bytes 98320 | tf_op jit(solution)/shard_map/reduce_scatter | solution.py:71
  182.6 1.7 fusion.79
  184.3 1.3 collective-permute-start.1
  185.6 5.5 %collective-permute-done.1 = f32[3,32,256]{2,1,0:T(8,128)} collective-permute-done((f32[3,32,256]{2,1,0:T(8,128)}, f32[3,32,256]{2,1,0:T(8,128)}, u32[]{:S(2)}, u32[]{:S(2)}) %collective-permute-start.1) | collective-permute-done | bytes 98336 | tf_op jit(solution)/shard_map/ppermute | solution.py:13
  191.1 1.0 multiply_reduce_fusion.5
  192.2 1.0 fusion.94
  193.2 15.8 %all_gather.18 = f32[3,256,256]{2,1,0:T(8,128)S(1)} all-gather(f32[3,32,256]{2,1,0:T(8,128)S(1)} %fusion.94), channel_id=1, replica_groups=mesh['block'=4,'tok'=8] {'tok'}, dimensions={1}, use_global_device_ids=true | all-gather | bytes 884736 | tf_op jit(solution)/shard_map/all_gather | solution.py:67
  209.1 1.4 conditional.6
  209.1 0.6 broadcast.93.clone
  209.7 0.7 broadcast.93
  210.5 1.0 fusion.84
  211.5 35.1 %reduce-scatter.12.cloned.1.call-done = f32[3,32,256]{2,1,0:T(8,128)} async-done(((f32[3,256,256]{2,1,0:T(8,128)}), f32[3,32,256]{2,1,0:T(8,128)}) %reduce-scatter.12.cloned.1.call-update) | async-done | bytes 98320 | tf_op jit(solution)/shard_map/reduce_scatter | solution.py:71
  246.6 1.7 fusion.82
  248.3 1.3 collective-permute-start.2
  249.6 5.5 %collective-permute-done.2 = f32[3,32,256]{2,1,0:T(8,128)} collective-permute-done((f32[3,32,256]{2,1,0:T(8,128)}, f32[3,32,256]{2,1,0:T(8,128)}, u32[]{:S(2)}, u32[]{:S(2)}) %collective-permute-start.2) | collective-permute-done | bytes 98336 | tf_op jit(solution)/shard_map/ppermute | solution.py:13
  255.1 1.0 multiply_reduce_fusion.4
  256.2 1.0 fusion.95
  257.3 15.8 %all_gather.19 = f32[3,256,256]{2,1,0:T(8,128)S(1)} all-gather(f32[3,32,256]{2,1,0:T(8,128)S(1)} %fusion.95), channel_id=1, replica_groups=mesh['block'=4,'tok'=8] {'tok'}, dimensions={1}, use_global_device_ids=true | all-gather | bytes 884736 | tf_op jit(solution)/shard_map/all_gather | solution.py:67
  273.1 6.2 %conditional.7 = (f32[3,256,256]{2,1,0:T(8,128)S(1)}, f32[128,256]{1,0:T(8,128)}, f32[128,256]{1,0:T(8,128)}, f32[128]{0:T(128)S(1)}) conditional(s32[]{:T(128)} %convert_element_type.12, () %tuple.51, (f32[3,256,256]{2,1,0:T(8,128)S(1)}, f32[128,256]{1,0:T(8,128)S(1)}, f32[128,256]{1,0:T(8,128)S(1)}, f32[128,256]{1,0:T(8,128)S(1)}, ...), branch_computations={%region_19.20_spmd, %region_20.22_spmd} | conditional | flops 1209499520 | bytes 10880032 | solution.py:68
  275.5 0.9 multiply_reduce_fusion.3
  276.9 1.1 convolution_add_fusion.13
  278.0 0.4 convolution_bitcast_fusion.9
  278.4 0.4 convolution_bitcast_fusion.10
  278.8 0.4 convolution_bitcast_fusion.11
  279.3 1.0 fusion.83
  280.3 0.9 copy-done.40
  281.6 0.5 copy-done.38
  282.1 1.0 convolution_add_fusion.16
  283.2 0.5 broadcast_select_fusion.3
  283.7 1.7 select_select_fusion
  285.4 23.9 %reduce-scatter.14.cloned.1.call-done = f32[3,32,256]{2,1,0:T(8,128)} async-done(((f32[3,256,256]{2,1,0:T(8,128)}), f32[3,32,256]{2,1,0:T(8,128)}) %reduce-scatter.14.cloned.1.call-update) | async-done | bytes 98320 | tf_op jit(solution)/shard_map/reduce_scatter | solution.py:71
  309.3 1.7 fusion.72
  (122 shorter events, 5.7 us)
Async XLA Ops:
  7.2 23.4 %copy-start = (f32[128,256]{1,0:T(8,128)S(1)}, f32[128,256]{1,0:T(8,128)}, u32[]{:S(2)}) copy-start(f32[128,256]{1,0:T(8,128)} %param.15) | copy-start | bytes 393220
  7.2 56.5 %reduce-scatter.6.cloned.1.call-start = ((), (), s32[]{:S(2)}) async-start(), calls=%async_computation.5 | async-start | bytes 884736 | tf_op jit(solution)/shard_map/reduce_scatter | solution.py:49
  7.9 17.6 %copy-start.43 = (f32[128,256]{1,0:T(8,128)S(1)}, f32[128,256]{1,0:T(8,128)}, u32[]{:S(2)}) copy-start(f32[128,256]{1,0:T(8,128)} %param.17) | copy-start | bytes 393220
  25.5 0.9 copy-start.1
  28.2 0.9 copy-start.10
  28.2 0.9 copy-start.15
  30.5 88.4 %reduce-scatter.8.cloned.1.call-start = ((), (), s32[]{:S(2)}) async-start(), calls=%async_computation.6 | async-start | bytes 884736 | tf_op jit(solution)/shard_map/reduce_scatter | solution.py:71
  30.8 0.9 copy-start.42
  31.7 1.3 copy-start.37
  32.6 0.7 copy-start.39
  33.7 30.0 %copy-start.20 = (f32[1,3,32,256]{3,2,1,0:T(8,128)S(1)}, f32[1,3,32,256]{3,2,1,0:T(8,128)}, u32[]{:S(2)}) copy-start(f32[1,3,32,256]{3,2,1,0:T(8,128)} %param.19) | copy-start | bytes 294916
  63.6 1.1 copy-start.41
  63.7 17.2 %copy-start.33 = (f32[128,256]{1,0:T(8,128)S(1)}, f32[128,256]{1,0:T(8,128)}, u32[]{:S(2)}) copy-start(f32[128,256]{1,0:T(8,128)} %get-tuple-element.291) | copy-start | bytes 393220
  64.8 16.0 %copy-start.21 = (f32[128,256]{1,0:T(8,128)S(1)}, f32[128,256]{1,0:T(8,128)}, u32[]{:S(2)}) copy-start(f32[128,256]{1,0:T(8,128)} %get-tuple-element.312) | copy-start | bytes 393220
  64.8 16.0 %copy-start.25 = (f32[128,256]{1,0:T(8,128)S(1)}, f32[128,256]{1,0:T(8,128)}, u32[]{:S(2)}) copy-start(f32[128,256]{1,0:T(8,128)} %get-tuple-element.314) | copy-start | bytes 393220
  64.8 16.0 %copy-start.29 = (f32[128,256]{1,0:T(8,128)S(1)}, f32[128,256]{1,0:T(8,128)}, u32[]{:S(2)}) copy-start(f32[128,256]{1,0:T(8,128)} %get-tuple-element.315) | copy-start | bytes 393220
  64.9 15.9 %copy-start.2 = (f32[256,256]{1,0:T(8,128)S(1)}, f32[256,256]{1,0:T(8,128)}, u32[]{:S(2)}) copy-start(f32[256,256]{1,0:T(8,128)} %get-tuple-element.308) | copy-start | bytes 786436
  64.9 15.9 %copy-start.6 = (f32[256,256]{1,0:T(8,128)S(1)}, f32[256,256]{1,0:T(8,128)}, u32[]{:S(2)}) copy-start(f32[256,256]{1,0:T(8,128)} %get-tuple-element.309) | copy-start | bytes 786436
  64.9 15.9 %copy-start.11 = (f32[128,256]{1,0:T(8,128)S(1)}, f32[128,256]{1,0:T(8,128)}, u32[]{:S(2)}) copy-start(f32[128,256]{1,0:T(8,128)} %copy-done.10) | copy-start | bytes 393220
  65.0 15.9 %copy-start.16 = (f32[128,256]{1,0:T(8,128)S(1)}, f32[128,256]{1,0:T(8,128)}, u32[]{:S(2)}) copy-start(f32[128,256]{1,0:T(8,128)} %copy-done.15) | copy-start | bytes 393220
  80.8 0.7 copy-start.44
  83.9 98.7 %reduce-scatter.10.cloned.1.call-start = ((), (), s32[]{:S(2)}) async-start(), calls=%async_computation.7 | async-start | bytes 884736 | tf_op jit(solution)/shard_map/reduce_scatter | solution.py:71
  120.6 6.8 %collective-permute-start = (f32[3,32,256]{2,1,0:T(8,128)}, f32[3,32,256]{2,1,0:T(8,128)}, u32[]{:S(2)}, u32[]{:S(2)}) collective-permute-start(f32[3,32,256]{2,1,0:T(8,128)} %fusion.76), channel_id=1, source_target_pairs={{8,0},{16,8},{24,16},{9,1},{17,9},{25,17},{10,2},{18,10},{26,18},{... | collective-permute-start | bytes 294920 | tf_op jit(solution)/shard_map/ppermute | solution.py:13
  127.4 17.9 %copy-start.34 = (f32[128,256]{1,0:T(8,128)S(1)}, f32[128,256]{1,0:T(8,128)}, u32[]{:S(2)}) copy-start(f32[128,256]{1,0:T(8,128)} %get-tuple-element.291) | copy-start | bytes 393220
  128.5 16.9 %copy-start.22 = (f32[128,256]{1,0:T(8,128)S(1)}, f32[128,256]{1,0:T(8,128)}, u32[]{:S(2)}) copy-start(f32[128,256]{1,0:T(8,128)} %get-tuple-element.312) | copy-start | bytes 393220
  128.5 16.9 %copy-start.26 = (f32[128,256]{1,0:T(8,128)S(1)}, f32[128,256]{1,0:T(8,128)}, u32[]{:S(2)}) copy-start(f32[128,256]{1,0:T(8,128)} %get-tuple-element.314) | copy-start | bytes 393220
  128.5 16.9 %copy-start.30 = (f32[128,256]{1,0:T(8,128)S(1)}, f32[128,256]{1,0:T(8,128)}, u32[]{:S(2)}) copy-start(f32[128,256]{1,0:T(8,128)} %get-tuple-element.315) | copy-start | bytes 393220
  129.6 15.8 %copy-start.3 = (f32[256,256]{1,0:T(8,128)S(1)}, f32[256,256]{1,0:T(8,128)}, u32[]{:S(2)}) copy-start(f32[256,256]{1,0:T(8,128)} %get-tuple-element.308) | copy-start | bytes 786436
  129.6 15.8 %copy-start.7 = (f32[256,256]{1,0:T(8,128)S(1)}, f32[256,256]{1,0:T(8,128)}, u32[]{:S(2)}) copy-start(f32[256,256]{1,0:T(8,128)} %get-tuple-element.309) | copy-start | bytes 786436
  129.6 15.8 %copy-start.12 = (f32[128,256]{1,0:T(8,128)S(1)}, f32[128,256]{1,0:T(8,128)}, u32[]{:S(2)}) copy-start(f32[128,256]{1,0:T(8,128)} %copy-done.10) | copy-start | bytes 393220
  129.6 15.8 %copy-start.17 = (f32[128,256]{1,0:T(8,128)S(1)}, f32[128,256]{1,0:T(8,128)}, u32[]{:S(2)}) copy-start(f32[128,256]{1,0:T(8,128)} %copy-done.15) | copy-start | bytes 393220
  148.1 98.6 %reduce-scatter.12.cloned.1.call-start = ((), (), s32[]{:S(2)}) async-start(), calls=%async_computation.8 | async-start | bytes 884736 | tf_op jit(solution)/shard_map/reduce_scatter | solution.py:71
  184.3 6.8 %collective-permute-start.1 = (f32[3,32,256]{2,1,0:T(8,128)}, f32[3,32,256]{2,1,0:T(8,128)}, u32[]{:S(2)}, u32[]{:S(2)}) collective-permute-start(f32[3,32,256]{2,1,0:T(8,128)} %fusion.79), channel_id=1, source_target_pairs={{8,0},{16,8},{24,16},{9,1},{17,9},{25,17},{10,2},{18,10},{26,18},{... | collective-permute-start | bytes 294920 | tf_op jit(solution)/shard_map/ppermute | solution.py:13
  191.1 17.9 %copy-start.35 = (f32[128,256]{1,0:T(8,128)S(1)}, f32[128,256]{1,0:T(8,128)}, u32[]{:S(2)}) copy-start(f32[128,256]{1,0:T(8,128)} %get-tuple-element.291) | copy-start | bytes 393220
  192.1 16.9 %copy-start.23 = (f32[128,256]{1,0:T(8,128)S(1)}, f32[128,256]{1,0:T(8,128)}, u32[]{:S(2)}) copy-start(f32[128,256]{1,0:T(8,128)} %get-tuple-element.312) | copy-start | bytes 393220
  192.1 16.9 %copy-start.27 = (f32[128,256]{1,0:T(8,128)S(1)}, f32[128,256]{1,0:T(8,128)}, u32[]{:S(2)}) copy-start(f32[128,256]{1,0:T(8,128)} %get-tuple-element.314) | copy-start | bytes 393220
  192.2 16.9 %copy-start.31 = (f32[128,256]{1,0:T(8,128)S(1)}, f32[128,256]{1,0:T(8,128)}, u32[]{:S(2)}) copy-start(f32[128,256]{1,0:T(8,128)} %get-tuple-element.315) | copy-start | bytes 393220
  193.2 15.8 %copy-start.4 = (f32[256,256]{1,0:T(8,128)S(1)}, f32[256,256]{1,0:T(8,128)}, u32[]{:S(2)}) copy-start(f32[256,256]{1,0:T(8,128)} %get-tuple-element.308) | copy-start | bytes 786436
  193.2 15.8 %copy-start.8 = (f32[256,256]{1,0:T(8,128)S(1)}, f32[256,256]{1,0:T(8,128)}, u32[]{:S(2)}) copy-start(f32[256,256]{1,0:T(8,128)} %get-tuple-element.309) | copy-start | bytes 786436
  193.2 15.8 %copy-start.13 = (f32[128,256]{1,0:T(8,128)S(1)}, f32[128,256]{1,0:T(8,128)}, u32[]{:S(2)}) copy-start(f32[128,256]{1,0:T(8,128)} %copy-done.10) | copy-start | bytes 393220
  193.2 15.8 %copy-start.18 = (f32[128,256]{1,0:T(8,128)S(1)}, f32[128,256]{1,0:T(8,128)}, u32[]{:S(2)}) copy-start(f32[128,256]{1,0:T(8,128)} %copy-done.15) | copy-start | bytes 393220
  211.5 97.8 %reduce-scatter.14.cloned.1.call-start = ((), (), s32[]{:S(2)}) async-start(), calls=%async_computation.9 | async-start | bytes 884736 | tf_op jit(solution)/shard_map/reduce_scatter | solution.py:71
  248.3 6.8 %collective-permute-start.2 = (f32[3,32,256]{2,1,0:T(8,128)}, f32[3,32,256]{2,1,0:T(8,128)}, u32[]{:S(2)}, u32[]{:S(2)}) collective-permute-start(f32[3,32,256]{2,1,0:T(8,128)} %fusion.82), channel_id=1, source_target_pairs={{8,0},{16,8},{24,16},{9,1},{17,9},{25,17},{10,2},{18,10},{26,18},{... | collective-permute-start | bytes 294920 | tf_op jit(solution)/shard_map/ppermute | solution.py:13
  255.1 17.9 %copy-start.36 = (f32[128,256]{1,0:T(8,128)S(1)}, f32[128,256]{1,0:T(8,128)}, u32[]{:S(2)}) copy-start(f32[128,256]{1,0:T(8,128)} %get-tuple-element.291) | copy-start | bytes 393220
  256.2 16.9 %copy-start.24 = (f32[128,256]{1,0:T(8,128)S(1)}, f32[128,256]{1,0:T(8,128)}, u32[]{:S(2)}) copy-start(f32[128,256]{1,0:T(8,128)} %get-tuple-element.312) | copy-start | bytes 393220
  256.2 16.9 %copy-start.28 = (f32[128,256]{1,0:T(8,128)S(1)}, f32[128,256]{1,0:T(8,128)}, u32[]{:S(2)}) copy-start(f32[128,256]{1,0:T(8,128)} %get-tuple-element.314) | copy-start | bytes 393220
  256.2 16.9 %copy-start.32 = (f32[128,256]{1,0:T(8,128)S(1)}, f32[128,256]{1,0:T(8,128)}, u32[]{:S(2)}) copy-start(f32[128,256]{1,0:T(8,128)} %get-tuple-element.315) | copy-start | bytes 393220
  257.3 15.8 %copy-start.5 = (f32[256,256]{1,0:T(8,128)S(1)}, f32[256,256]{1,0:T(8,128)}, u32[]{:S(2)}) copy-start(f32[256,256]{1,0:T(8,128)} %get-tuple-element.308) | copy-start | bytes 786436
  257.3 15.8 %copy-start.9 = (f32[256,256]{1,0:T(8,128)S(1)}, f32[256,256]{1,0:T(8,128)}, u32[]{:S(2)}) copy-start(f32[256,256]{1,0:T(8,128)} %get-tuple-element.309) | copy-start | bytes 786436
  257.3 15.8 %copy-start.14 = (f32[128,256]{1,0:T(8,128)S(1)}, f32[128,256]{1,0:T(8,128)}, u32[]{:S(2)}) copy-start(f32[128,256]{1,0:T(8,128)} %copy-done.10) | copy-start | bytes 393220
  257.3 15.8 %copy-start.19 = (f32[128,256]{1,0:T(8,128)S(1)}, f32[128,256]{1,0:T(8,128)}, u32[]{:S(2)}) copy-start(f32[128,256]{1,0:T(8,128)} %copy-done.15) | copy-start | bytes 393220
  280.3 0.9 copy-start.40
  281.2 0.9 copy-start.38
Sparse Core Ops, SparseCore 0:
  30.6 33.0 reduce-scatter.5
  84.0 34.8 reduce-scatter.7
  148.2 34.3 reduce-scatter.9
  211.6 34.9 reduce-scatter.11
  280.4 28.8 reduce-scatter.13
where the time goes:
time: 318 us
  waiting for transfers between devices  174 us (55%)
  blocking collectives  80.7 us (25%)
  other arithmetic  22.3 us (7%)
  between operations  14.5 us (5%)
  matrix products  12.5 us (4%)
  local copies, waits for them, and re-layouts  8.76 us (3%)
  starting transfers between devices  4.04 us (1%)
    reduce_scatter x4, waiting for transfers between devices, per_device(): lax.psum_scatter(second_state + apply_state, 'tok', scatter_dimension=1,...  128 us
    all_gather x4, blocking collectives, per_device(): d_grad = lax.all_gather(-d_shifted, 'tok', axis=1, tiled=True)  63.2 us
    reduce_scatter x1, waiting for transfers between devices, per_device(): lax.psum_scatter(grad_part, 'tok', scatter_dimension=1, tiled=True)  29.1 us
    all_gather x1, blocking collectives, per_device(): gathered = lax.all_gather(own_rows, 'tok', axis=1, tiled=True)  17.5 us
    ppermute x3, waiting for transfers between devices, from_behind(): return lax.ppermute(array, axis, pairs)  16.6 us
  transfers between devices with their start and end apart: 8, of which 8 were waited for; matrix products, arithmetic and copies ran while one was open for 2% of the time, Pallas kernels for 0%

commit v1 on v0

--- a/solution.py
+++ b/solution.py
@@ -64,7 +64,24 @@
     for section in range(groups):
         active = position == groups - 1 - section
         d_shifted, direct = norm_adjoint(incoming, shifted, own_rows, row_norm, new_norm)
-        d_grad = lax.all_gather(-d_shifted, "tok", axis=1, tiled=True)
+        x = -d_shifted
+        ways, here, step = (lax.axis_size("tok"), lax.axis_index("tok"), x.shape[1])
+        shape = [n * ways if d == 1 else n for d, n in enumerate(x.shape)]
+        full = lax.dynamic_update_slice_in_dim(jnp.zeros(shape, x.dtype), x, here * step, axis=1)
+        going_up = going_down = x
+        for far in range(1, ways // 2 + 1):
+            going_up = lax.ppermute(going_up, "tok", [(d, (d + 1) % ways) for d in range(ways)])
+            full = lax.dynamic_update_slice_in_dim(
+                full, going_up, (here - far) % ways * step, axis=1
+            )
+            if 2 * far < ways:
+                going_down = lax.ppermute(
+                    going_down, "tok", [(d, (d - 1) % ways) for d in range(ways)]
+                )
+                full = lax.dynamic_update_slice_in_dim(
+                    full, going_down, (here + far) % ways * step, axis=1
+                )
+        d_grad = full
         second_state, second_keys, second_values, second_rates = lax.cond(
             active, lambda cot: second_back(cot), lambda cot: zero_back, d_grad
         )

time: 318 us -> 436 us (1.37)
  waiting for transfers between devices: 174 us -> 290 us
  blocking collectives: 80.7 us -> 17.5 us
  starting transfers between devices: 4.04 us -> 41.1 us
  local copies, waits for them, and re-layouts: 8.76 us -> 39 us
    all_gather x4 -> x0, blocking collectives: 63.2 us -> none  [per_device(): d_grad = lax.all_gather(-d_shifted, 'tok', axis=1, tiled=True)]
    reduce_scatter x4, waiting for transfers between devices: 128 us -> 192 us  [per_device(): lax.psum_scatter(second_state + apply_state, 'tok', scatter_dimension=1,...]
    ppermute x0 -> x28, waiting for transfers between devices: none -> 51.3 us  [the longest x16 50.4 us: per_device(): lax.ppermute(going_up, 'tok', [(d, (d + 1) % ways) for d in range(ways)])]
    ppermute x0 -> x28, starting transfers between devices: none -> 37 us  [the longest x12 36.8 us: per_device(): lax.ppermute(going_down, 'tok', [(d, (d - 1) % ways) for d in range(ways)])]
    another operation x9 -> x22, local copies, waits for them, and re-layouts: 3.94 us -> 14.6 us
    dynamic_update_slice x0 -> x8, local copies, waits for them, and re-layouts: none -> 9.11 us  [the longest x4 4.53 us: per_device(): lax.dynamic_update_slice_in_dim(full, going_up, (here - far) % ways * ste...]
    unnamed x90 -> x140, local copies, waits for them, and re-layouts: 3.79 us -> 10.8 us
  transfers between devices with their start and end apart: 8 -> 36, of which waited for: 8 -> 27; matrix products, arithmetic and copies ran while one was open for 2% -> 2% of each run, Pallas kernels for 0% -> 0%
where the time goes in v1:
time: 436 us; the launch traced here: 435 us
  waiting for transfers between devices  290 us (67%)
  starting transfers between devices  41.1 us (9%)
  local copies, waits for them, and re-layouts  39 us (9%)
  other arithmetic  18.6 us (4%)
  blocking collectives  17.5 us (4%)
  between operations  14.6 us (3%)
  matrix products  13.3 us (3%)
    reduce_scatter x4, waiting for transfers between devices, per_device(): lax.psum_scatter(second_state + apply_state, 'tok', scatter_dimension=1,...  192 us
    ppermute x16, waiting for transfers between devices, per_device(): lax.ppermute(going_up, 'tok', [(d, (d + 1) % ways) for d in range(ways)])  50.4 us
    ppermute x12, starting transfers between devices, per_device(): lax.ppermute(going_down, 'tok', [(d, (d - 1) % ways) for d in range(ways)])  36.8 us
    reduce_scatter x1, waiting for transfers between devices, per_device(): lax.psum_scatter(grad_part, 'tok', scatter_dimension=1, tiled=True)  31.7 us
    all_gather x1, blocking collectives, per_device(): gathered = lax.all_gather(own_rows, 'tok', axis=1, tiled=True)  17.5 us
    ppermute x3, waiting for transfers between devices, from_behind(): return lax.ppermute(array, axis, pairs)  15.6 us
    another operation x22, local copies, waits for them, and re-layouts  14.6 us
    unnamed x140, local copies, waits for them, and re-layouts  10.8 us
  transfers between devices with their start and end apart: 36, of which 27 were waited for; matrix products, arithmetic and copies ran while one was open for 2% of the time, Pallas kernels for 0%

profile of v1, /device:TPU:0, one launch (start us, length us, event | category | flops | bytes accessed | tf_op | source)
XLA Modules:
  0.0 435.1 jit_solution(9383541837243958455)
XLA Ops:
  7.9 17.5 %all-gather = f32[1,3,256,256]{3,2,1,0:T(8,128)S(1)} all-gather(f32[1,3,32,256]{3,2,1,0:T(8,128)} %param.19), channel_id=2, replica_groups=mesh['block'=4,'tok'=8] {'tok'}, dimensions={2}, use_global_device_ids=true | all-gather | bytes 884736 | tf_op jit(solution)/shard_map/all_gather | solution.py:45
  27.1 1.2 multiply_add_fusion.12
  32.2 31.7 %reduce-scatter.6.cloned.1.call-done = f32[3,32,256]{2,1,0:T(8,128)} async-done(((f32[3,256,256]{2,1,0:T(8,128)}), f32[3,32,256]{2,1,0:T(8,128)}) %reduce-scatter.6.cloned.1.call-update) | async-done | bytes 98320 | tf_op jit(solution)/shard_map/reduce_scatter | solution.py:49
  66.5 2.9 collective-permute-start.1
  69.4 1.8 collective-permute-done
  71.8 3.4 collective-permute-start.3
  75.2 1.9 collective-permute-done.2
  77.6 3.6 collective-permute-start.5
  81.2 1.8 collective-permute-done.4
  83.4 5.4 %collective-permute-done.6 = f32[3,32,256]{2,1,0:T(8,128)S(1)} collective-permute-done((f32[3,32,256]{2,1,0:T(8,128)S(1)}, f32[3,32,256]{2,1,0:T(8,128)S(1)}, u32[]{:S(2)}, u32[]{:S(2)}) %collective-permute-start.6) | collective-permute-done | bytes 98336 | tf_op jit(solution)/shard_map/ppermute | solution.py:73
  89.5 2.3 conditional.4
  91.8 2.1 fusion.34
  94.0 56.8 %reduce-scatter.8.cloned.1.call-done = f32[3,32,256]{2,1,0:T(8,128)} async-done(((f32[3,256,256]{2,1,0:T(8,128)}), f32[3,32,256]{2,1,0:T(8,128)}) %reduce-scatter.8.cloned.1.call-update) | async-done | bytes 98320 | tf_op jit(solution)/shard_map/reduce_scatter | solution.py:88
  150.8 1.1 fusion.24
  151.8 1.3 collective-permute-start.7
  153.1 5.2 %collective-permute-done.7 = f32[3,32,256]{2,1,0:T(8,128)S(1)} collective-permute-done((f32[3,32,256]{2,1,0:T(8,128)S(1)}, f32[3,32,256]{2,1,0:T(8,128)S(1)}, u32[]{:S(2)}, u32[]{:S(2)}) %collective-permute-start.7) | collective-permute-done | bytes 98336 | tf_op jit(solution)/shard_map/ppermute | solution.py:13
  159.7 3.0 collective-permute-start.9
  162.7 2.7 collective-permute-done.8
  166.0 2.9 collective-permute-start.11
  169.0 2.4 collective-permute-done.10
  172.0 3.1 collective-permute-start.13
  175.1 2.2 collective-permute-done.12
  177.6 5.9 %collective-permute-done.14 = f32[3,32,256]{2,1,0:T(8,128)} collective-permute-done((f32[3,32,256]{2,1,0:T(8,128)}, f32[3,32,256]{2,1,0:T(8,128)}, u32[]{:S(2)}, u32[]{:S(2)}) %collective-permute-start.14) | collective-permute-done | bytes 98336 | tf_op jit(solution)/shard_map/ppermute | solution.py:73
  183.5 2.3 conditional.5
  185.8 2.1 fusion.33
  188.0 55.6 %reduce-scatter.10.cloned.1.call-done = f32[3,32,256]{2,1,0:T(8,128)} async-done(((f32[3,256,256]{2,1,0:T(8,128)}), f32[3,32,256]{2,1,0:T(8,128)}) %reduce-scatter.10.cloned.1.call-update) | async-done | bytes 98320 | tf_op jit(solution)/shard_map/reduce_scatter | solution.py:88
  243.7 1.1 fusion.27
  244.7 1.3 collective-permute-start.15
  246.0 5.2 %collective-permute-done.15 = f32[3,32,256]{2,1,0:T(8,128)S(1)} collective-permute-done((f32[3,32,256]{2,1,0:T(8,128)S(1)}, f32[3,32,256]{2,1,0:T(8,128)S(1)}, u32[]{:S(2)}, u32[]{:S(2)}) %collective-permute-start.15) | collective-permute-done | bytes 98336 | tf_op jit(solution)/shard_map/ppermute | solution.py:13
  252.7 3.0 collective-permute-start.17
  255.6 2.7 collective-permute-done.16
  259.0 2.9 collective-permute-start.19
  261.9 2.4 collective-permute-done.18
  265.0 3.0 collective-permute-start.21
  268.0 2.3 collective-permute-done.20
  270.5 5.9 %collective-permute-done.22 = f32[3,32,256]{2,1,0:T(8,128)} collective-permute-done((f32[3,32,256]{2,1,0:T(8,128)}, f32[3,32,256]{2,1,0:T(8,128)}, u32[]{:S(2)}, u32[]{:S(2)}) %collective-permute-start.22) | collective-permute-done | bytes 98336 | tf_op jit(solution)/shard_map/ppermute | solution.py:73
  276.5 2.3 conditional.6
  278.8 2.1 fusion.32
  281.0 56.4 %reduce-scatter.12.cloned.1.call-done = f32[3,32,256]{2,1,0:T(8,128)} async-done(((f32[3,256,256]{2,1,0:T(8,128)}), f32[3,32,256]{2,1,0:T(8,128)}) %reduce-scatter.12.cloned.1.call-update) | async-done | bytes 98320 | tf_op jit(solution)/shard_map/reduce_scatter | solution.py:88
  337.4 1.1 fusion.30
  338.5 1.3 collective-permute-start.23
  339.8 5.2 %collective-permute-done.23 = f32[3,32,256]{2,1,0:T(8,128)S(1)} collective-permute-done((f32[3,32,256]{2,1,0:T(8,128)S(1)}, f32[3,32,256]{2,1,0:T(8,128)S(1)}, u32[]{:S(2)}, u32[]{:S(2)}) %collective-permute-start.23) | collective-permute-done | bytes 98336 | tf_op jit(solution)/shard_map/ppermute | solution.py:13
  346.4 3.0 collective-permute-start.25
  349.4 2.7 collective-permute-done.24
  352.7 2.9 collective-permute-start.27
  355.6 2.4 collective-permute-done.26
  358.7 3.0 collective-permute-start.29
  361.7 2.3 collective-permute-done.28
  364.2 5.9 %collective-permute-done.30 = f32[3,32,256]{2,1,0:T(8,128)} collective-permute-done((f32[3,32,256]{2,1,0:T(8,128)}, f32[3,32,256]{2,1,0:T(8,128)}, u32[]{:S(2)}, u32[]{:S(2)}) %collective-permute-start.30) | collective-permute-done | bytes 98336 | tf_op jit(solution)/shard_map/ppermute | solution.py:73
  370.2 27.8 %conditional.7 = (f32[3,256,256]{2,1,0:T(8,128)S(1)}, f32[128,256]{1,0:T(8,128)}, f32[128]{0:T(128)S(1)}, f32[128,256]{1,0:T(8,128)S(1)}) conditional(s32[]{:T(128)} %convert_element_type.12, () %tuple.67, (f32[3,32,256]{2,1,0:T(8,128)}, s32[]{:T(128)}, f32[3,32,256]{2,1,0:T(8,128)}, s32[]{:T(128)}, f32[3,32,256]{2,1,0:T(8,128)}, ...), branch_computations={%region_19.20_spmd, %region_20.22_spmd} | conditional | flops 1209499520 | bytes 25822780 | solution.py:85
  371.3 1.7 copy.71
  378.6 1.1 dynamic_update_slice.248
  379.7 1.1 dynamic_update_slice.249
  380.8 1.1 dynamic_update_slice.250
  382.0 1.1 dynamic_update_slice.251
  383.1 1.1 dynamic_update_slice.252
  384.3 1.1 dynamic_update_slice.253
  385.4 1.1 dynamic_update_slice.254
  386.6 1.1 dynamic_update_slice.255
  387.7 1.3 fusion.11
  400.9 1.0 convolution_add_fusion.12
  402.4 1.7 select_select_fusion
  404.2 22.7 %reduce-scatter.14.cloned.1.call-done = f32[3,32,256]{2,1,0:T(8,128)} async-done(((f32[3,256,256]{2,1,0:T(8,128)}), f32[3,32,256]{2,1,0:T(8,128)}) %reduce-scatter.14.cloned.1.call-update) | async-done | bytes 98320 | tf_op jit(solution)/shard_map/reduce_scatter | solution.py:88
  426.9 1.7 fusion.20
  (279 shorter events, 45.1 us)
Async XLA Ops:
  7.2 56.8 %reduce-scatter.6.cloned.1.call-start = ((), (), s32[]{:S(2)}) async-start(), calls=%async_computation.5 | async-start | bytes 884736 | tf_op jit(solution)/shard_map/reduce_scatter | solution.py:49
  26.7 62.7 %copy-start.6 = (f32[128,256]{1,0:T(8,128)}, f32[128,256]{1,0:T(8,128)S(1)}, u32[]{:S(2)}) copy-start(f32[128,256]{1,0:T(8,128)S(1)} %fusion.55) | copy-start | bytes 393220
  27.1 62.3 %copy-start.10 = (f32[128,256]{1,0:T(8,128)}, f32[128,256]{1,0:T(8,128)S(1)}, u32[]{:S(2)}) copy-start(f32[128,256]{1,0:T(8,128)S(1)} %fusion.51) | copy-start | bytes 393220
  28.3 61.1 %copy-start.14 = (f32[128,256]{1,0:T(8,128)}, f32[128,256]{1,0:T(8,128)S(1)}, u32[]{:S(2)}) copy-start(f32[128,256]{1,0:T(8,128)S(1)} %get-tuple-element.1332) | copy-start | bytes 393220
  28.3 61.1 %copy-start.18 = (f32[128,256]{1,0:T(8,128)}, f32[128,256]{1,0:T(8,128)S(1)}, u32[]{:S(2)}) copy-start(f32[128,256]{1,0:T(8,128)S(1)} %get-tuple-element.1333) | copy-start | bytes 393220
  28.3 61.1 %copy-start.22 = (f32[128,256]{1,0:T(8,128)}, f32[128,256]{1,0:T(8,128)S(1)}, u32[]{:S(2)}) copy-start(f32[128,256]{1,0:T(8,128)S(1)} %get-tuple-element.1369) | copy-start | bytes 393220
  30.8 119.9 %reduce-scatter.8.cloned.1.call-start = ((), (), s32[]{:S(2)}) async-start(), calls=%async_computation.6 | async-start | bytes 884736 | tf_op jit(solution)/shard_map/reduce_scatter | solution.py:88
  31.1 51.8 %copy-start.36 = (f32[128,256]{1,0:T(8,128)}, f32[128,256]{1,0:T(8,128)S(1)}, u32[]{:S(2)}) copy-start(f32[128,256]{1,0:T(8,128)S(1)} %fusion.54) | copy-start | bytes 393220
  31.4 45.7 %copy-start.55 = (f32[128,256]{1,0:T(8,128)}, f32[128,256]{1,0:T(8,128)S(1)}, u32[]{:S(2)}) copy-start(f32[128,256]{1,0:T(8,128)S(1)} %fusion.56) | copy-start | bytes 393220
  31.5 32.5 %copy-start.31 = (f32[1,3,32,256]{3,2,1,0:T(8,128)S(1)}, f32[1,3,32,256]{3,2,1,0:T(8,128)}, u32[]{:S(2)}) copy-start(f32[1,3,32,256]{3,2,1,0:T(8,128)} %param.19) | copy-start | bytes 294916
  31.5 32.5 %copy-start.90 = (f32[3,32,256]{2,1,0:T(8,128)S(1)}, f32[3,32,256]{2,1,0:T(8,128)}, u32[]{:S(2)}) copy-start(f32[3,32,256]{2,1,0:T(8,128)} %param.21) | copy-start | bytes 294916
  65.1 6.0 %collective-permute-start = (f32[3,32,256]{2,1,0:T(8,128)S(1)}, f32[3,32,256]{2,1,0:T(8,128)S(1)}, u32[]{:S(2)}, u32[]{:S(2)}) collective-permute-start(f32[3,32,256]{2,1,0:T(8,128)S(1)} %fusion.40), channel_id=1, source_target_pairs={{0,1},{1,2},{2,3},{3,4},{4,5},{5,6},{6,7},{7,0},{8,9},{9,10},{10,1... | collective-permute-start | bytes 294920 | tf_op jit(solution)/shard_map/ppermute | solution.py:73
  66.5 5.3 %collective-permute-start.1 = (f32[3,32,256]{2,1,0:T(8,128)S(1)}, f32[3,32,256]{2,1,0:T(8,128)S(1)}, u32[]{:S(2)}, u32[]{:S(2)}) collective-permute-start(f32[3,32,256]{2,1,0:T(8,128)S(1)} %fusion.40), channel_id=1, source_target_pairs={{0,7},{1,0},{2,1},{3,2},{4,3},{5,4},{6,5},{7,6},{8,15},{9,8},{10,9... | collective-permute-start | bytes 294920 | tf_op jit(solution)/shard_map/ppermute | solution.py:78
  71.1 6.0 %collective-permute-start.2 = (f32[3,32,256]{2,1,0:T(8,128)S(1)}, f32[3,32,256]{2,1,0:T(8,128)S(1)}, u32[]{:S(2)}, u32[]{:S(2)}) collective-permute-start(f32[3,32,256]{2,1,0:T(8,128)S(1)} %collective-permute-done), channel_id=1, source_target_pairs={{0,1},{1,2},{2,3},{3,4},{4,5},{5,6},{6,7},{7,0},{8,9},{9,10},{10,1... | collective-permute-start | bytes 294920 | tf_op jit(solution)/shard_map/ppermute | solution.py:73
  71.8 5.8 %collective-permute-start.3 = (f32[3,32,256]{2,1,0:T(8,128)S(1)}, f32[3,32,256]{2,1,0:T(8,128)S(1)}, u32[]{:S(2)}, u32[]{:S(2)}) collective-permute-start(f32[3,32,256]{2,1,0:T(8,128)S(1)} %collective-permute-done.1), channel_id=1, source_target_pairs={{0,7},{1,0},{2,1},{3,2},{4,3},{5,4},{6,5},{7,6},{8,15},{9,8},{10,9... | collective-permute-start | bytes 294920 | tf_op jit(solution)/shard_map/ppermute | solution.py:78
  77.1 5.8 %collective-permute-start.4 = (f32[3,32,256]{2,1,0:T(8,128)S(1)}, f32[3,32,256]{2,1,0:T(8,128)S(1)}, u32[]{:S(2)}, u32[]{:S(2)}) collective-permute-start(f32[3,32,256]{2,1,0:T(8,128)S(1)} %collective-permute-done.2), channel_id=1, source_target_pairs={{0,1},{1,2},{2,3},{3,4},{4,5},{5,6},{6,7},{7,0},{8,9},{9,10},{10,1... | collective-permute-start | bytes 294920 | tf_op jit(solution)/shard_map/ppermute | solution.py:73
  77.6 5.8 %collective-permute-start.5 = (f32[3,32,256]{2,1,0:T(8,128)S(1)}, f32[3,32,256]{2,1,0:T(8,128)S(1)}, u32[]{:S(2)}, u32[]{:S(2)}) collective-permute-start(f32[3,32,256]{2,1,0:T(8,128)S(1)} %collective-permute-done.3), channel_id=1, source_target_pairs={{0,7},{1,0},{2,1},{3,2},{4,3},{5,4},{6,5},{7,6},{8,15},{9,8},{10,9... | collective-permute-start | bytes 294920 | tf_op jit(solution)/shard_map/ppermute | solution.py:78
  83.0 5.8 %collective-permute-start.6 = (f32[3,32,256]{2,1,0:T(8,128)S(1)}, f32[3,32,256]{2,1,0:T(8,128)S(1)}, u32[]{:S(2)}, u32[]{:S(2)}) collective-permute-start(f32[3,32,256]{2,1,0:T(8,128)S(1)} %collective-permute-done.4), channel_id=1, source_target_pairs={{0,1},{1,2},{2,3},{3,4},{4,5},{5,6},{6,7},{7,0},{8,9},{9,10},{10,1... | collective-permute-start | bytes 294920 | tf_op jit(solution)/shard_map/ppermute | solution.py:73
  93.9 56.8 %copy-start.32 = (f32[1,3,32,256]{3,2,1,0:T(8,128)S(1)}, f32[1,3,32,256]{3,2,1,0:T(8,128)}, u32[]{:S(2)}) copy-start(f32[1,3,32,256]{3,2,1,0:T(8,128)} %param.19) | copy-start | bytes 294916
  93.9 56.8 %copy-start.91 = (f32[3,32,256]{2,1,0:T(8,128)S(1)}, f32[3,32,256]{2,1,0:T(8,128)}, u32[]{:S(2)}) copy-start(f32[3,32,256]{2,1,0:T(8,128)} %param.21) | copy-start | bytes 294916
  93.9 149.7 %reduce-scatter.10.cloned.1.call-start = ((), (), s32[]{:S(2)}) async-start(), calls=%async_computation.7 | async-start | bytes 884736 | tf_op jit(solution)/shard_map/reduce_scatter | solution.py:88
  150.7 32.7 %copy-start.19 = (f32[128,256]{1,0:T(8,128)S(1)}, f32[128,256]{1,0:T(8,128)}, u32[]{:S(2)}) copy-start(f32[128,256]{1,0:T(8,128)} %copy-done.18) | copy-start | bytes 393220
  150.7 32.7 %copy-start.23 = (f32[128,256]{1,0:T(8,128)S(1)}, f32[128,256]{1,0:T(8,128)}, u32[]{:S(2)}) copy-start(f32[128,256]{1,0:T(8,128)} %copy-done.22) | copy-start | bytes 393220
  150.7 32.7 %copy-start.42 = (f32[128,256]{1,0:T(8,128)S(1)}, f32[128,256]{1,0:T(8,128)}, u32[]{:S(2)}) copy-start(f32[128,256]{1,0:T(8,128)} %get-tuple-element.1352) | copy-start | bytes 393220
  151.8 6.5 %collective-permute-start.7 = (f32[3,32,256]{2,1,0:T(8,128)S(1)}, f32[3,32,256]{2,1,0:T(8,128)S(1)}, u32[]{:S(2)}, u32[]{:S(2)}) collective-permute-start(f32[3,32,256]{2,1,0:T(8,128)S(1)} %fusion.24), channel_id=1, source_target_pairs={{8,0},{16,8},{24,16},{9,1},{17,9},{25,17},{10,2},{18,10},{26,18},{... | collective-permute-start | bytes 294920 | tf_op jit(solution)/shard_map/ppermute | solution.py:13
  158.3 25.1 %copy-start.15 = (f32[128,256]{1,0:T(8,128)S(1)}, f32[128,256]{1,0:T(8,128)}, u32[]{:S(2)}) copy-start(f32[128,256]{1,0:T(8,128)} %copy-done.14) | copy-start | bytes 393220
  159.1 6.3 %collective-permute-start.8 = (f32[3,32,256]{2,1,0:T(8,128)S(1)}, f32[3,32,256]{2,1,0:T(8,128)S(1)}, u32[]{:S(2)}, u32[]{:S(2)}) collective-permute-start(f32[3,32,256]{2,1,0:T(8,128)S(1)} %fusion.41), channel_id=1, source_target_pairs={{0,1},{1,2},{2,3},{3,4},{4,5},{5,6},{6,7},{7,0},{8,9},{9,10},{10,1... | collective-permute-start | bytes 294920 | tf_op jit(solution)/shard_map/ppermute | solution.py:73
  159.7 5.7 %collective-permute-start.9 = (f32[3,32,256]{2,1,0:T(8,128)S(1)}, f32[3,32,256]{2,1,0:T(8,128)S(1)}, u32[]{:S(2)}, u32[]{:S(2)}) collective-permute-start(f32[3,32,256]{2,1,0:T(8,128)S(1)} %fusion.41), channel_id=1, source_target_pairs={{0,7},{1,0},{2,1},{3,2},{4,3},{5,4},{6,5},{7,6},{8,15},{9,8},{10,9... | collective-permute-start | bytes 294920 | tf_op jit(solution)/shard_map/ppermute | solution.py:78
  165.4 6.0 %collective-permute-start.10 = (f32[3,32,256]{2,1,0:T(8,128)S(1)}, f32[3,32,256]{2,1,0:T(8,128)S(1)}, u32[]{:S(2)}, u32[]{:S(2)}) collective-permute-start(f32[3,32,256]{2,1,0:T(8,128)S(1)} %collective-permute-done.8), channel_id=1, source_target_pairs={{0,1},{1,2},{2,3},{3,4},{4,5},{5,6},{6,7},{7,0},{8,9},{9,10},{10,1... | collective-permute-start | bytes 294920 | tf_op jit(solution)/shard_map/ppermute | solution.py:73
  166.0 5.3 %collective-permute-start.11 = (f32[3,32,256]{2,1,0:T(8,128)S(1)}, f32[3,32,256]{2,1,0:T(8,128)}, u32[]{:S(2)}, u32[]{:S(2)}) collective-permute-start(f32[3,32,256]{2,1,0:T(8,128)S(1)} %collective-permute-done.9), channel_id=1, source_target_pairs={{0,7},{1,0},{2,1},{3,2},{4,3},{5,4},{6,5},{7,6},{8,15},{9,8},{10,9... | collective-permute-start | bytes 294920 | tf_op jit(solution)/shard_map/ppermute | solution.py:78
  171.4 5.9 %collective-permute-start.12 = (f32[3,32,256]{2,1,0:T(8,128)S(1)}, f32[3,32,256]{2,1,0:T(8,128)}, u32[]{:S(2)}, u32[]{:S(2)}) collective-permute-start(f32[3,32,256]{2,1,0:T(8,128)S(1)} %collective-permute-done.10), channel_id=1, source_target_pairs={{0,1},{1,2},{2,3},{3,4},{4,5},{5,6},{6,7},{7,0},{8,9},{9,10},{10,1... | collective-permute-start | bytes 294920 | tf_op jit(solution)/shard_map/ppermute | solution.py:73
  172.0 5.6 %collective-permute-start.13 = (f32[3,32,256]{2,1,0:T(8,128)}, f32[3,32,256]{2,1,0:T(8,128)}, u32[]{:S(2)}, u32[]{:S(2)}) collective-permute-start(f32[3,32,256]{2,1,0:T(8,128)} %collective-permute-done.11), channel_id=1, source_target_pairs={{0,7},{1,0},{2,1},{3,2},{4,3},{5,4},{6,5},{7,6},{8,15},{9,8},{10,9... | collective-permute-start | bytes 294920 | tf_op jit(solution)/shard_map/ppermute | solution.py:78
  177.3 6.2 %collective-permute-start.14 = (f32[3,32,256]{2,1,0:T(8,128)}, f32[3,32,256]{2,1,0:T(8,128)}, u32[]{:S(2)}, u32[]{:S(2)}) collective-permute-start(f32[3,32,256]{2,1,0:T(8,128)} %collective-permute-done.12), channel_id=1, source_target_pairs={{0,1},{1,2},{2,3},{3,4},{4,5},{5,6},{6,7},{7,0},{8,9},{9,10},{10,1... | collective-permute-start | bytes 294920 | tf_op jit(solution)/shard_map/ppermute | solution.py:73
  188.0 55.7 %copy-start.33 = (f32[1,3,32,256]{3,2,1,0:T(8,128)S(1)}, f32[1,3,32,256]{3,2,1,0:T(8,128)}, u32[]{:S(2)}) copy-start(f32[1,3,32,256]{3,2,1,0:T(8,128)} %param.19) | copy-start | bytes 294916
  188.0 55.7 %copy-start.87 = (f32[3,32,256]{2,1,0:T(8,128)S(1)}, f32[3,32,256]{2,1,0:T(8,128)}, u32[]{:S(2)}) copy-start(f32[3,32,256]{2,1,0:T(8,128)} %copy-done.86) | copy-start | bytes 294916
  188.0 149.4 %reduce-scatter.12.cloned.1.call-start = ((), (), s32[]{:S(2)}) async-start(), calls=%async_computation.8 | async-start | bytes 884736 | tf_op jit(solution)/shard_map/reduce_scatter | solution.py:88
  243.6 32.8 %copy-start.20 = (f32[128,256]{1,0:T(8,128)S(1)}, f32[128,256]{1,0:T(8,128)}, u32[]{:S(2)}) copy-start(f32[128,256]{1,0:T(8,128)} %copy-done.18) | copy-start | bytes 393220
  243.6 32.8 %copy-start.24 = (f32[128,256]{1,0:T(8,128)S(1)}, f32[128,256]{1,0:T(8,128)}, u32[]{:S(2)}) copy-start(f32[128,256]{1,0:T(8,128)} %copy-done.22) | copy-start | bytes 393220
  243.7 32.8 %copy-start.43 = (f32[128,256]{1,0:T(8,128)S(1)}, f32[128,256]{1,0:T(8,128)}, u32[]{:S(2)}) copy-start(f32[128,256]{1,0:T(8,128)} %get-tuple-element.1352) | copy-start | bytes 393220
  244.7 6.5 %collective-permute-start.15 = (f32[3,32,256]{2,1,0:T(8,128)S(1)}, f32[3,32,256]{2,1,0:T(8,128)S(1)}, u32[]{:S(2)}, u32[]{:S(2)}) collective-permute-start(f32[3,32,256]{2,1,0:T(8,128)S(1)} %fusion.27), channel_id=1, source_target_pairs={{8,0},{16,8},{24,16},{9,1},{17,9},{25,17},{10,2},{18,10},{26,18},{... | collective-permute-start | bytes 294920 | tf_op jit(solution)/shard_map/ppermute | solution.py:13
  251.3 25.2 %copy-start.16 = (f32[128,256]{1,0:T(8,128)S(1)}, f32[128,256]{1,0:T(8,128)}, u32[]{:S(2)}) copy-start(f32[128,256]{1,0:T(8,128)} %copy-done.14) | copy-start | bytes 393220
  251.9 24.5 %copy-start.12 = (f32[128,256]{1,0:T(8,128)S(1)}, f32[128,256]{1,0:T(8,128)}, u32[]{:S(2)}) copy-start(f32[128,256]{1,0:T(8,128)} %copy-done.10) | copy-start | bytes 393220
  252.0 6.3 %collective-permute-start.16 = (f32[3,32,256]{2,1,0:T(8,128)S(1)}, f32[3,32,256]{2,1,0:T(8,128)S(1)}, u32[]{:S(2)}, u32[]{:S(2)}) collective-permute-start(f32[3,32,256]{2,1,0:T(8,128)S(1)} %fusion.42), channel_id=1, source_target_pairs={{0,1},{1,2},{2,3},{3,4},{4,5},{5,6},{6,7},{7,0},{8,9},{9,10},{10,1... | collective-permute-start | bytes 294920 | tf_op jit(solution)/shard_map/ppermute | solution.py:73
  252.7 5.7 %collective-permute-start.17 = (f32[3,32,256]{2,1,0:T(8,128)S(1)}, f32[3,32,256]{2,1,0:T(8,128)S(1)}, u32[]{:S(2)}, u32[]{:S(2)}) collective-permute-start(f32[3,32,256]{2,1,0:T(8,128)S(1)} %fusion.42), channel_id=1, source_target_pairs={{0,7},{1,0},{2,1},{3,2},{4,3},{5,4},{6,5},{7,6},{8,15},{9,8},{10,9... | collective-permute-start | bytes 294920 | tf_op jit(solution)/shard_map/ppermute | solution.py:78
  258.3 6.0 %collective-permute-start.18 = (f32[3,32,256]{2,1,0:T(8,128)S(1)}, f32[3,32,256]{2,1,0:T(8,128)S(1)}, u32[]{:S(2)}, u32[]{:S(2)}) collective-permute-start(f32[3,32,256]{2,1,0:T(8,128)S(1)} %collective-permute-done.16), channel_id=1, source_target_pairs={{0,1},{1,2},{2,3},{3,4},{4,5},{5,6},{6,7},{7,0},{8,9},{9,10},{10,1... | collective-permute-start | bytes 294920 | tf_op jit(solution)/shard_map/ppermute | solution.py:73
  259.0 5.3 %collective-permute-start.19 = (f32[3,32,256]{2,1,0:T(8,128)S(1)}, f32[3,32,256]{2,1,0:T(8,128)}, u32[]{:S(2)}, u32[]{:S(2)}) collective-permute-start(f32[3,32,256]{2,1,0:T(8,128)S(1)} %collective-permute-done.17), channel_id=1, source_target_pairs={{0,7},{1,0},{2,1},{3,2},{4,3},{5,4},{6,5},{7,6},{8,15},{9,8},{10,9... | collective-permute-start | bytes 294920 | tf_op jit(solution)/shard_map/ppermute | solution.py:78
  264.3 5.9 %collective-permute-start.20 = (f32[3,32,256]{2,1,0:T(8,128)S(1)}, f32[3,32,256]{2,1,0:T(8,128)}, u32[]{:S(2)}, u32[]{:S(2)}) collective-permute-start(f32[3,32,256]{2,1,0:T(8,128)S(1)} %collective-permute-done.18), channel_id=1, source_target_pairs={{0,1},{1,2},{2,3},{3,4},{4,5},{5,6},{6,7},{7,0},{8,9},{9,10},{10,1... | collective-permute-start | bytes 294920 | tf_op jit(solution)/shard_map/ppermute | solution.py:73
  265.0 5.6 %collective-permute-start.21 = (f32[3,32,256]{2,1,0:T(8,128)}, f32[3,32,256]{2,1,0:T(8,128)}, u32[]{:S(2)}, u32[]{:S(2)}) collective-permute-start(f32[3,32,256]{2,1,0:T(8,128)} %collective-permute-done.19), channel_id=1, source_target_pairs={{0,7},{1,0},{2,1},{3,2},{4,3},{5,4},{6,5},{7,6},{8,15},{9,8},{10,9... | collective-permute-start | bytes 294920 | tf_op jit(solution)/shard_map/ppermute | solution.py:78
  270.3 6.2 %collective-permute-start.22 = (f32[3,32,256]{2,1,0:T(8,128)}, f32[3,32,256]{2,1,0:T(8,128)}, u32[]{:S(2)}, u32[]{:S(2)}) collective-permute-start(f32[3,32,256]{2,1,0:T(8,128)} %collective-permute-done.20), channel_id=1, source_target_pairs={{0,1},{1,2},{2,3},{3,4},{4,5},{5,6},{6,7},{7,0},{8,9},{9,10},{10,1... | collective-permute-start | bytes 294920 | tf_op jit(solution)/shard_map/ppermute | solution.py:73
  280.9 56.5 %copy-start.34 = (f32[1,3,32,256]{3,2,1,0:T(8,128)S(1)}, f32[1,3,32,256]{3,2,1,0:T(8,128)}, u32[]{:S(2)}) copy-start(f32[1,3,32,256]{3,2,1,0:T(8,128)} %param.19) | copy-start | bytes 294916
  280.9 56.5 %copy-start.89 = (f32[3,32,256]{2,1,0:T(8,128)S(1)}, f32[3,32,256]{2,1,0:T(8,128)}, u32[]{:S(2)}) copy-start(f32[3,32,256]{2,1,0:T(8,128)} %copy-done.88) | copy-start | bytes 294916
  280.9 146.0 %reduce-scatter.14.cloned.1.call-start = ((), (), s32[]{:S(2)}) async-start(), calls=%async_computation.9 | async-start | bytes 884736 | tf_op jit(solution)/shard_map/reduce_scatter | solution.py:88
  337.4 32.7 %copy-start.21 = (f32[128,256]{1,0:T(8,128)S(1)}, f32[128,256]{1,0:T(8,128)}, u32[]{:S(2)}) copy-start(f32[128,256]{1,0:T(8,128)} %copy-done.18) | copy-start | bytes 393220
  337.4 32.7 %copy-start.25 = (f32[128,256]{1,0:T(8,128)S(1)}, f32[128,256]{1,0:T(8,128)}, u32[]{:S(2)}) copy-start(f32[128,256]{1,0:T(8,128)} %copy-done.22) | copy-start | bytes 393220
  337.4 32.7 %copy-start.44 = (f32[128,256]{1,0:T(8,128)S(1)}, f32[128,256]{1,0:T(8,128)}, u32[]{:S(2)}) copy-start(f32[128,256]{1,0:T(8,128)} %get-tuple-element.1352) | copy-start | bytes 393220
  338.5 6.5 %collective-permute-start.23 = (f32[3,32,256]{2,1,0:T(8,128)S(1)}, f32[3,32,256]{2,1,0:T(8,128)S(1)}, u32[]{:S(2)}, u32[]{:S(2)}) collective-permute-start(f32[3,32,256]{2,1,0:T(8,128)S(1)} %fusion.30), channel_id=1, source_target_pairs={{8,0},{16,8},{24,16},{9,1},{17,9},{25,17},{10,2},{18,10},{26,18},{... | collective-permute-start | bytes 294920 | tf_op jit(solution)/shard_map/ppermute | solution.py:13
  345.0 25.1 %copy-start.17 = (f32[128,256]{1,0:T(8,128)S(1)}, f32[128,256]{1,0:T(8,128)}, u32[]{:S(2)}) copy-start(f32[128,256]{1,0:T(8,128)} %copy-done.14) | copy-start | bytes 393220
  345.8 6.3 %collective-permute-start.24 = (f32[3,32,256]{2,1,0:T(8,128)S(1)}, f32[3,32,256]{2,1,0:T(8,128)S(1)}, u32[]{:S(2)}, u32[]{:S(2)}) collective-permute-start(f32[3,32,256]{2,1,0:T(8,128)S(1)} %fusion.43), channel_id=1, source_target_pairs={{0,1},{1,2},{2,3},{3,4},{4,5},{5,6},{6,7},{7,0},{8,9},{9,10},{10,1... | collective-permute-start | bytes 294920 | tf_op jit(solution)/shard_map/ppermute | solution.py:73
  346.4 5.6 %collective-permute-start.25 = (f32[3,32,256]{2,1,0:T(8,128)S(1)}, f32[3,32,256]{2,1,0:T(8,128)S(1)}, u32[]{:S(2)}, u32[]{:S(2)}) collective-permute-start(f32[3,32,256]{2,1,0:T(8,128)S(1)} %fusion.43), channel_id=1, source_target_pairs={{0,7},{1,0},{2,1},{3,2},{4,3},{5,4},{6,5},{7,6},{8,15},{9,8},{10,9... | collective-permute-start | bytes 294920 | tf_op jit(solution)/shard_map/ppermute | solution.py:78
  352.0 6.0 %collective-permute-start.26 = (f32[3,32,256]{2,1,0:T(8,128)S(1)}, f32[3,32,256]{2,1,0:T(8,128)S(1)}, u32[]{:S(2)}, u32[]{:S(2)}) collective-permute-start(f32[3,32,256]{2,1,0:T(8,128)S(1)} %collective-permute-done.24), channel_id=1, source_target_pairs={{0,1},{1,2},{2,3},{3,4},{4,5},{5,6},{6,7},{7,0},{8,9},{9,10},{10,1... | collective-permute-start | bytes 294920 | tf_op jit(solution)/shard_map/ppermute | solution.py:73
  352.7 5.3 %collective-permute-start.27 = (f32[3,32,256]{2,1,0:T(8,128)S(1)}, f32[3,32,256]{2,1,0:T(8,128)}, u32[]{:S(2)}, u32[]{:S(2)}) collective-permute-start(f32[3,32,256]{2,1,0:T(8,128)S(1)} %collective-permute-done.25), channel_id=1, source_target_pairs={{0,7},{1,0},{2,1},{3,2},{4,3},{5,4},{6,5},{7,6},{8,15},{9,8},{10,9... | collective-permute-start | bytes 294920 | tf_op jit(solution)/shard_map/ppermute | solution.py:78
  358.0 5.9 %collective-permute-start.28 = (f32[3,32,256]{2,1,0:T(8,128)S(1)}, f32[3,32,256]{2,1,0:T(8,128)}, u32[]{:S(2)}, u32[]{:S(2)}) collective-permute-start(f32[3,32,256]{2,1,0:T(8,128)S(1)} %collective-permute-done.26), channel_id=1, source_target_pairs={{0,1},{1,2},{2,3},{3,4},{4,5},{5,6},{6,7},{7,0},{8,9},{9,10},{10,1... | collective-permute-start | bytes 294920 | tf_op jit(solution)/shard_map/ppermute | solution.py:73
  358.7 5.6 %collective-permute-start.29 = (f32[3,32,256]{2,1,0:T(8,128)}, f32[3,32,256]{2,1,0:T(8,128)}, u32[]{:S(2)}, u32[]{:S(2)}) collective-permute-start(f32[3,32,256]{2,1,0:T(8,128)} %collective-permute-done.27), channel_id=1, source_target_pairs={{0,7},{1,0},{2,1},{3,2},{4,3},{5,4},{6,5},{7,6},{8,15},{9,8},{10,9... | collective-permute-start | bytes 294920 | tf_op jit(solution)/shard_map/ppermute | solution.py:78
  364.0 6.2 %collective-permute-start.30 = (f32[3,32,256]{2,1,0:T(8,128)}, f32[3,32,256]{2,1,0:T(8,128)}, u32[]{:S(2)}, u32[]{:S(2)}) collective-permute-start(f32[3,32,256]{2,1,0:T(8,128)} %collective-permute-done.28), channel_id=1, source_target_pairs={{0,1},{1,2},{2,3},{3,4},{4,5},{5,6},{6,7},{7,0},{8,9},{9,10},{10,1... | collective-permute-start | bytes 294920 | tf_op jit(solution)/shard_map/ppermute | solution.py:73
  (60 other events, 385.3 us)
Sparse Core Ops, SparseCore 0:
  30.9 33.0 reduce-scatter.5
  94.0 56.6 reduce-scatter.7
  188.1 55.4 reduce-scatter.9
  281.1 56.3 reduce-scatter.11
  399.1 27.7 reduce-scatter.13
